TPU v7x, 32 devices: a whole 2x2x4 slice. The times are simulated.
32 devices in a mesh: groups: 2 (over x), segment: 4 (over y, core), head: 4 (over z).
Axes of the slice: x: 2, y: 2, z: 4, core: 2. Of those that a mesh axis runs over, the one named last changes fastest.
Arguments:
- token_ids: int32 [6, 256], P('groups'), parts along dimension 0, may hold values from 0 to 18991, as said below
- embed_table: bfloat16 [18992, 256], P(('segment', 'head')), may hold values from -6 to 6
- arriving: bfloat16 [8, 256, 256], P(('groups', 'segment')), parts along dimension 0, may hold values from -16 to 16
- returning: bfloat16 [8, 256, 256], P(('groups', 'segment')), parts along dimension 0, may hold values from -6 to 6
- stashed: bfloat16 [8, 3, 256, 256], P(('groups', 'segment')), parts along dimension 0, may hold values from -16 to 16
- seed_grad: bfloat16 [6, 256, 256], P('groups'), parts along dimension 0, may hold values from -6 to 6
- expand: bfloat16 [4, 256, 2048], P('segment'), may hold values from -0.375 to 0.375
- compress: bfloat16 [4, 2048, 256], P('segment'), may hold values from -0.125 to 0.125
- norm_gain: float32 [4, 2048], P('segment'), may hold values from 0.1 to 1.9
- w_query: bfloat16 [4, 2048, 4096], P('segment', None, 'head'), may hold values from -0.125 to 0.125
- key_weight: bfloat16 [4, 2048, 512], P('segment'), may hold values from -0.125 to 0.125
- value_weight: bfloat16 [4, 2048, 512], P('segment'), may hold values from -0.125 to 0.125
- w_out: bfloat16 [4, 4096, 2048], P('segment', 'head'), may hold values from -0.09375 to 0.09375
Outputs:
- sent_forward: bfloat16 [8, 3, 256, 256], P(('groups', 'segment'), None, 'head'), parts along dimension 0
- sent_backward: bfloat16 [8, 3, 256, 256], P(('groups', 'segment'), None, 'head'), parts along dimension 0
There are 2 independent parts, one for each index of `groups`. A program takes and returns all parts, laid end to end along the dimension named above; an argument that names none is the same for every part. Nothing has to cross between parts.
Inputs may be any that keep to these rules, and one draw needn't show every extreme that they name: `token_ids`: every aligned block of 1187 ids is named by some token.
All inputs are finite; a program needn't handle non-finite values.
Results may differ from a plain program's by a relative error of at most 0.02.
Values may be sent and summed in bfloat16 or wider, within the bound.
A program may use at most 128 MiB of HBM per device.

v0:
```python
import math
import jax
import jax.numpy as jnp
from jax import lax
from jax.sharding import PartitionSpec as P

QUERY_HEADS = 32
KEY_VALUE_HEADS = 4
HEAD_SIZE = 128
EPS = 1e-06


def passed_along(x, axis, by):
    length = lax.axis_size(axis)
    pairs = [(i, i + by) for i in range(length) if 0 <= i + by < length]
    return lax.ppermute(x, axis, pairs)


def rms_scale(matrix):
    return lax.rsqrt(jnp.mean(matrix * matrix, axis=-1, keepdims=True) + EPS)


def precise(former, latter):
    return jnp.dot(
        former, latter, precision=lax.Precision.HIGHEST, preferred_element_type=jnp.float32
    )


def precise_back(former, latter):
    return lax.dot_general(
        former,
        latter,
        (((1,), (1,)), ((), ())),
        precision=lax.Precision.HIGHEST,
        preferred_element_type=jnp.float32,
    )


def narrow_back(former, latter):
    return lax.dot_general(
        former, latter, (((1,), (1,)), ((), ())), preferred_element_type=jnp.float32
    )


def norm_back(upstream_in, grad_hat):
    scaling = rms_scale(upstream_in)
    return scaling * grad_hat - upstream_in * scaling**3 * jnp.mean(
        grad_hat * upstream_in, axis=-1, keepdims=True
    )


def section_inputs(coeffs, expand_here, gain_here, query_here, key_here, value_here):
    row_count = coeffs.shape[0]
    hidden = jnp.dot(coeffs, expand_here, preferred_element_type=jnp.float32)
    scaling = rms_scale(hidden)
    normed = (hidden * scaling * gain_here).astype(jnp.bfloat16)
    queries = jnp.dot(normed, query_here, preferred_element_type=jnp.float32).reshape(
        row_count, -1, HEAD_SIZE
    )
    key_rows = jnp.dot(normed, key_here, preferred_element_type=jnp.float32).reshape(
        row_count, -1, HEAD_SIZE
    )
    values = (
        jnp.dot(normed, value_here, preferred_element_type=jnp.float32)
        .astype(jnp.bfloat16)
        .reshape(row_count, -1, HEAD_SIZE)
    )
    q_hat = (queries * rms_scale(queries)).astype(jnp.bfloat16)
    k_hat = (key_rows * rms_scale(key_rows)).astype(jnp.bfloat16)
    return (hidden, scaling, queries, key_rows, q_hat, k_hat, values)


def probabilities(q_hat, k_hat):
    row_count, head_count, head_width = q_hat.shape
    kv_heads = k_hat.shape[1]
    grouped = q_hat.reshape(row_count, kv_heads, head_count // kv_heads, head_width)
    scores = jnp.einsum(
        "iknd,jkd->knij", grouped, k_hat, preferred_element_type=jnp.float32
    ) / math.sqrt(head_width)
    causal = jnp.arange(row_count)[None, :] <= jnp.arange(row_count)[:, None]
    weights = jnp.where(causal, jnp.exp(scores), 0.0)
    return weights / jnp.sum(weights, axis=-1, keepdims=True)


def section_forward(coeffs, expand_here, gain_here, query_here, key_here, value_here, out_folded):
    hidden, scaling, queries, key_rows, q_hat, k_hat, values = section_inputs(
        coeffs, expand_here, gain_here, query_here, key_here, value_here
    )
    weights = probabilities(q_hat, k_hat)
    attended = jnp.einsum(
        "knij,jkd->iknd", weights.astype(jnp.bfloat16), values, preferred_element_type=jnp.float32
    )
    attended = attended.reshape(coeffs.shape[0], -1).astype(jnp.bfloat16)
    return jnp.dot(attended, out_folded, preferred_element_type=jnp.float32)


def section_backward(
    coeffs, grads, expand_here, gain_here, query_here, key_here, value_here, out_folded
):
    row_count = coeffs.shape[0]
    hidden, scaling, queries, key_rows, q_hat, k_hat, values = section_inputs(
        coeffs, expand_here, gain_here, query_here, key_here, value_here
    )
    weights = probabilities(q_hat, k_hat)
    head_count = queries.shape[1]
    kv_heads = key_rows.shape[1]
    query_group_size = head_count // kv_heads
    grad_attended = narrow_back(grads, out_folded).astype(jnp.bfloat16)
    grad_attended = grad_attended.reshape(row_count, kv_heads, query_group_size, HEAD_SIZE)
    grad_weights = jnp.einsum(
        "iknd,jkd->knij", grad_attended, values, preferred_element_type=jnp.float32
    )
    grad_scores = (
        weights
        * (grad_weights - jnp.sum(grad_weights * weights, axis=-1, keepdims=True))
        / math.sqrt(HEAD_SIZE)
    )
    grad_scores = grad_scores.astype(jnp.bfloat16)
    grouped = q_hat.reshape(row_count, kv_heads, query_group_size, HEAD_SIZE)
    grad_qhat = jnp.einsum(
        "knij,jkd->iknd", grad_scores, k_hat, preferred_element_type=jnp.float32
    ).reshape(row_count, head_count, HEAD_SIZE)
    grad_khat = jnp.einsum(
        "knij,iknd->jkd", grad_scores, grouped, preferred_element_type=jnp.float32
    )
    grad_values = jnp.einsum(
        "knij,iknd->jkd",
        weights.astype(jnp.bfloat16),
        grad_attended,
        preferred_element_type=jnp.float32,
    )
    grad_values = grad_values.reshape(row_count, -1).astype(jnp.bfloat16)
    grad_queries = norm_back(queries, grad_qhat).reshape(row_count, -1).astype(jnp.bfloat16)
    grad_keys = norm_back(key_rows, grad_khat).reshape(row_count, -1).astype(jnp.bfloat16)
    grad_normed = (
        narrow_back(grad_queries, query_here)
        + narrow_back(grad_keys, key_here)
        + narrow_back(grad_values, value_here)
    )
    weighted = grad_normed * gain_here
    grad_hidden = scaling * weighted - hidden * scaling**3 * jnp.mean(
        weighted * hidden, axis=-1, keepdims=True
    )
    return narrow_back(grad_hidden.astype(jnp.bfloat16), expand_here)


def shards(
    token_ids,
    embed_table,
    arriving,
    returning,
    stashed,
    seed_grad,
    expand,
    compress,
    norm_gain,
    w_query,
    key_weight,
    value_weight,
    w_out,
):
    segment_index = lax.axis_index("segment")
    last_segment = lax.axis_size("segment") - 1
    head_index = lax.axis_index("head")
    heads_here = w_query.shape[2] // HEAD_SIZE
    query_group_size = QUERY_HEADS // KEY_VALUE_HEADS
    kv_here = (heads_here + query_group_size - 1) // query_group_size
    first_kv = head_index * heads_here // query_group_size
    expand_here = expand[0]
    gain_here = norm_gain[0]
    query_here = w_query[0]
    key_here = lax.dynamic_slice_in_dim(key_weight[0], first_kv * HEAD_SIZE, kv_here * HEAD_SIZE, 1)
    value_here = lax.dynamic_slice_in_dim(
        value_weight[0], first_kv * HEAD_SIZE, kv_here * HEAD_SIZE, 1
    )
    basis_folded = jnp.dot(expand_here, compress[0], preferred_element_type=jnp.float32)
    out_folded = jnp.dot(w_out[0], compress[0], preferred_element_type=jnp.float32).astype(
        jnp.bfloat16
    )
    table_rows = embed_table.shape[0]
    local_ids = token_ids.reshape(-1) - lax.axis_index(("segment", "head")) * table_rows
    inside = (local_ids >= 0) & (local_ids < table_rows)
    looked = jnp.take(embed_table, jnp.clip(local_ids, 0, table_rows - 1), axis=0).astype(
        jnp.float32
    )
    picked = jnp.where(inside[:, None], looked, 0.0)
    embedded = lax.psum(picked, ("segment", "head")).astype(jnp.bfloat16)
    tick_count = token_ids.shape[0]
    span_rows = token_ids.shape[1]
    embedded = embedded.reshape(tick_count, span_rows, -1)
    share_rows = span_rows // lax.axis_size("head")
    share_start = head_index * share_rows
    forward_recv = arriving[0]
    backward_recv = returning[0]
    history = []
    forward_shares = []
    backward_shares = []
    for tick_index in range(tick_count):
        more_ticks = tick_index + 1 < tick_count
        forward_in = jnp.where(segment_index == 0, embedded[tick_index], forward_recv)
        backward_in = jnp.where(segment_index == last_segment, seed_grad[tick_index], backward_recv)
        history.append(forward_in)
        delay_ticks = 2 * (last_segment - segment_index)
        replay = stashed[0, tick_index]
        for earlier in range(tick_index + 1):
            replay = jnp.where(delay_ticks == tick_index - earlier, history[earlier], replay)
        partial_value = section_forward(
            forward_in, expand_here, gain_here, query_here, key_here, value_here, out_folded
        )
        direct = precise(forward_in.astype(jnp.float32), basis_folded)
        summed = lax.psum_scatter(
            partial_value.astype(jnp.bfloat16), "head", scatter_dimension=0, tiled=True
        ).astype(jnp.float32)
        own_rows = (summed + lax.dynamic_slice_in_dim(direct, share_start, share_rows, 0)).astype(
            jnp.bfloat16
        )
        forward_shares.append(own_rows)
        if more_ticks:
            arrived = passed_along(own_rows, "segment", 1)
            forward_recv = lax.all_gather(arrived, "head", axis=0, tiled=True)
        partial_back = section_backward(
            replay,
            backward_in,
            expand_here,
            gain_here,
            query_here,
            key_here,
            value_here,
            out_folded,
        )
        direct_back = precise_back(backward_in.astype(jnp.float32), basis_folded)
        summed_back = lax.psum_scatter(
            partial_back.astype(jnp.bfloat16), "head", scatter_dimension=0, tiled=True
        ).astype(jnp.float32)
        own_back = (
            summed_back + lax.dynamic_slice_in_dim(direct_back, share_start, share_rows, 0)
        ).astype(jnp.bfloat16)
        backward_shares.append(own_back)
        if more_ticks:
            arrived_back = passed_along(own_back, "segment", -1)
            backward_recv = lax.all_gather(arrived_back, "head", axis=0, tiled=True)
    sent_forward = jnp.stack(forward_shares)[None]
    sent_backward = jnp.stack(backward_shares)[None]
    return (sent_forward, sent_backward)


def solution(mesh):
    return jax.shard_map(
        shards,
        mesh=mesh,
        in_specs=(
            P("groups", None),
            P(("segment", "head"), None),
            P(("groups", "segment"), None, None),
            P(("groups", "segment"), None, None),
            P(("groups", "segment"), None, None, None),
            P("groups", None, None),
            P("segment", None, None),
            P("segment", None, None),
            P("segment", None),
            P("segment", None, "head"),
            P("segment", None, None),
            P("segment", None, None),
            P("segment", "head", None),
        ),
        out_specs=(
            P(("groups", "segment"), None, "head", None),
            P(("groups", "segment"), None, "head", None),
        ),
        check_vma=False,
    )
```

profile of v0, /device:TPU:0, one launch (start us, length us, event | category | flops | bytes accessed | tf_op | source)
XLA Modules:
  0.0 454.7 jit_solution(9600917615611538147)
XLA Ops:
  9.6 4.0 gather_fusion
  13.6 2.3 convert_select_fusion
  15.9 78.0 %all-reduce.1 = bf16[768,256]{1,0:T(8,128)(2,1)} all-reduce(f32[768,256]{1,0:T(8,128)} %convert_select_fusion), channel_id=1, replica_groups=mesh['groups'=2,'segment'=4,'head'=4] {'segment','head'}, use_global_device_ids=true, to_apply=%region_0.1 | all-reduce | flops 196608 | bytes 1179648 | tf_op jit(solution)/shard_map/psum | solution.py:187
  96.7 1.8 multiply_convert_fusion.5
  101.1 6.5 %copy.87 = bf16[1024,2048]{1,0:T(8,128)(2,1)} copy(bf16[1024,2048]{0,1:T(8,128)(2,1)} %bitcast.659) | data formatting | bytes 8388608 | tf_op jit(solution)/shard_map/dot_general | solution.py:57
  107.6 4.0 multiply_reduce_fusion.17
  111.7 2.0 fusion.32
  113.7 1.9 fusion.23
  115.7 3.7 convolution_convert_fusion.5
  119.4 2.2 convolution_convert_fusion.8
  123.4 2.7 multiply_reduce_fusion.5
  126.1 1.9 fusion.155
  129.0 2.3 convolution_convert_fusion.2
  131.3 9.0 %reduce-scatter.7.cloned.1.call-done = bf16[64,256]{1,0:T(8,128)(2,1)} async-done(((bf16[256,256]{1,0:T(8,128)(2,1)}), bf16[64,256]{1,0:T(8,128)(2,1)}) %reduce-scatter.7.cloned.1.call-update) | async-done | bytes 32784 | tf_op jit(solution)/shard_map/reduce_scatter | solution.py:211
  141.8 1.9 collective-permute-start
  144.2 2.0 copy.92
  146.1 13.8 %all_gather.12 = bf16[256,256]{1,0:T(8,128)(2,1)S(1)} all-gather(bf16[64,256]{1,0:T(8,128)(2,1)} %collective-permute-done), channel_id=1, replica_groups=mesh['groups'=2,'segment'=4,'head'=4] {'head'}, dimensions={0}, use_global_device_ids=true | all-gather | bytes 163840 | tf_op jit(solution)/shard_map/all_gather | solution.py:220
  167.8 2.3 multiply_reduce_fusion.12
  173.0 2.9 multiply_reduce_fusion.14
  177.1 2.5 fusion.24
  179.6 3.8 convolution_convert_fusion.4
  183.4 2.2 convolution_convert_fusion.7
  187.6 3.1 fusion.141
  192.2 12.4 %reduce-scatter.9.cloned.1.call-done = bf16[64,256]{1,0:T(8,128)(2,1)} async-done(((bf16[256,256]{1,0:T(8,128)(2,1)}), bf16[64,256]{1,0:T(8,128)(2,1)}) %reduce-scatter.9.cloned.1.call-update) | async-done | bytes 32784 | tf_op jit(solution)/shard_map/reduce_scatter | solution.py:211
  208.6 13.7 %all_gather.13 = bf16[256,256]{1,0:T(8,128)(2,1)S(1)} all-gather(bf16[64,256]{1,0:T(8,128)(2,1)S(1)} %collective-permute-done.1), channel_id=1, replica_groups=mesh['groups'=2,'segment'=4,'head'=4] {'head'}, dimensions={0}, use_global_device_ids=true | all-gather | bytes 163840 | tf_op jit(solution)/shard_map/all_gather | solution.py:220
  227.3 2.3 multiply_reduce_fusion.18
  232.2 3.3 fusion.31
  235.5 5.0 %fusion.19 = (f32[8,256]{1,0:T(8,128)}, f32[256,256,8]{1,0,2:T(8,128)}) fusion(f32[8,256]{1,0:T(8,128)S(1)} %get-tuple-element.5, f32[256,256,8]{1,0,2:T(8,128)} %fusion.141, pred[256,256]{0,1:T(8,128)(4,1)S(1)} %copy-done.28, bf16[256,2048]{1,0:T(8,128)(2,1)} %copy-done.13, bf16[1,2048,512]{2,1,0:T(8,128)(2,1)S(1)} %copy-done, s32[]{:T(128)S(6)} %select_n.142, ...), kind=kOutput, calls=%fused_computation.38 | convolution fusion | flops 271087616 | bytes 6373380 | tf_op jit(solution)/shard_map/iknd,jkd->knij/dot_general | solution.py:110
  240.4 4.1 convert_bitcast_fusion.2
  246.3 1.9 multiply_reduce_fusion.13
  248.2 2.9 multiply_reduce_fusion.15
  251.1 3.0 copy.65
  257.3 3.6 fusion.4
  260.9 2.9 convolution_add_fusion.5
  263.7 5.1 %multiply_reduce_fusion.4 = (f32[256]{0:T(256)S(1)}, f32[256,2048]{1,0:T(8,128)}) fusion(f32[256,2048]{1,0:T(8,128)} %get-tuple-element.49, f32[2048]{0:T(1024)S(1)} %bitcast.678, f32[256,2048]{1,0:T(8,128)} %convolution_add_fusion.5, bf16[1,2048,512]{2,1,0:T(8,128)(2,1)S(1)} %copy-done, s32[]{:T(128)S(6)} %select_n.142, ...), kind=kOutput, calls=%fused_computation.51 | convolution fusion | flops 270565120 | bytes 8397828 | tf_op jit(solution)/shard_map/dot_general | solution.py:40
  268.8 3.5 convolution_convert_fusion.11
  273.0 3.1 multiply_reduce_fusion.21
  276.1 16.2 %reduce-scatter.13.cloned.1.call-done = bf16[64,256]{1,0:T(8,128)(2,1)} async-done(((bf16[256,256]{1,0:T(8,128)(2,1)}), bf16[64,256]{1,0:T(8,128)(2,1)}) %reduce-scatter.13.cloned.1.call-update) | async-done | bytes 32784 | tf_op jit(solution)/shard_map/reduce_scatter | solution.py:232
  296.2 13.5 %all_gather.14 = bf16[256,256]{1,0:T(8,128)(2,1)S(1)} all-gather(bf16[64,256]{1,0:T(8,128)(2,1)S(1)} %collective-permute-done.2), channel_id=1, replica_groups=mesh['groups'=2,'segment'=4,'head'=4] {'head'}, dimensions={0}, use_global_device_ids=true | all-gather | bytes 163840 | tf_op jit(solution)/shard_map/all_gather | solution.py:241
  310.4 2.2 convolution_convert_fusion.1
  312.6 5.0 %fusion.15 = (f32[8,256]{1,0:T(8,128)}, f32[256,256,8]{1,0,2:T(8,128)}) fusion(f32[8,256]{1,0:T(8,128)} %get-tuple-element.6, f32[256,256,8]{1,0,2:T(8,128)} %copy-done.10, pred[256,256]{0,1:T(8,128)(4,1)S(1)} %copy-done.29, bf16[256,2048]{1,0:T(8,128)(2,1)} %copy-done.12, bf16[1,2048,512]{2,1,0:T(8,128)(2,1)S(1)} %copy-done, s32[]{:T(128)S(6)} %select_n.142, ...), kind=kOutput, calls=%fused_computation.32 | convolution fusion | flops 271087616 | bytes 6373380 | tf_op jit(solution)/shard_map/iknd,jkd->knij/dot_general | solution.py:110
  317.6 4.0 convert_bitcast_fusion.1
  323.3 1.9 multiply_reduce_fusion.11
  326.1 2.6 copy.71
  331.9 3.6 fusion.2
  335.5 2.9 convolution_add_fusion.3
  338.3 5.1 %multiply_reduce_fusion.2 = (f32[256]{0:T(256)S(1)}, f32[256,2048]{1,0:T(8,128)}) fusion(f32[256,2048]{1,0:T(8,128)} %copy-done.3, f32[2048]{0:T(1024)S(1)} %bitcast.679, f32[256,2048]{1,0:T(8,128)} %convolution_add_fusion.3, bf16[1,2048,512]{2,1,0:T(8,128)(2,1)S(1)} %copy-done, s32[]{:T(128)S(6)} %select_n.142, bf16[256,8,128]{2,1,0:T(8,128)(2,1)} %bitcast.671, ...), kind=kOutput, calls=%fused_computation.47 | convolution fusion | flops 270565120 | bytes 8397828 | tf_op jit(solution)/shard_map/dot_general | solution.py:40
  343.4 3.5 convolution_convert_fusion.10
  347.0 3.0 fusion.101
  350.1 2.0 fusion.195
  352.1 12.9 %reduce-scatter.15.cloned.1.call-done = bf16[64,256]{1,0:T(8,128)(2,1)} async-done(((bf16[256,256]{1,0:T(8,128)(2,1)}), bf16[64,256]{1,0:T(8,128)(2,1)}) %reduce-scatter.15.cloned.1.call-update) | async-done | bytes 32784 | tf_op jit(solution)/shard_map/reduce_scatter | solution.py:232
  367.4 1.9 fusion.268
  369.3 13.6 %all_gather.15 = bf16[256,256]{1,0:T(8,128)(2,1)S(1)} all-gather(bf16[64,256]{1,0:T(8,128)(2,1)S(1)} %collective-permute-done.3), channel_id=1, replica_groups=mesh['groups'=2,'segment'=4,'head'=4] {'head'}, dimensions={0}, use_global_device_ids=true | all-gather | bytes 163840 | tf_op jit(solution)/shard_map/all_gather | solution.py:241
  383.5 2.3 convolution_convert_fusion
  385.8 5.4 %fusion.11 = (f32[8,256]{1,0:T(8,128)S(1)}, f32[8,256]{1,0:T(8,128)S(1)}, f32[256,256,8]{1,0,2:T(8,128)}) fusion(f32[8,256]{1,0:T(8,128)S(1)} %copy-done.68, f32[256,256,8]{1,0,2:T(8,128)} %get-tuple-element.76, pred[256,256]{0,1:T(8,128)(4,1)S(1)} %copy-done.30, f32[256,256,8]{1,0,2:T(8,128)} %fusion.101, bf16[256,2048]{1,0:T(8,128)(2,1)} %copy-done.20, ...), kind=kOutput, calls=%fused_computation.26 | convolution fusion | flops 272658432 | bytes 8478724 | tf_op jit(solution)/shard_map/iknd,jkd->knij/dot_general | solution.py:110
  391.2 4.0 convert_bitcast_fusion
  398.6 3.8 convolution_convert_fusion.3
  402.3 2.7 copy.77
  405.0 2.2 convolution_convert_fusion.6
  409.1 3.6 fusion.6
  412.7 2.9 convolution_add_fusion.1
  415.6 5.1 %multiply_reduce_fusion = (f32[256]{0:T(256)S(1)}, f32[256,2048]{1,0:T(8,128)}) fusion(f32[256,2048]{1,0:T(8,128)} %copy-done.2, f32[2048]{0:T(1024)S(1)} %bitcast.680, f32[256,2048]{1,0:T(8,128)} %convolution_add_fusion.1, bf16[1,2048,512]{2,1,0:T(8,128)(2,1)S(1)} %copy-done, s32[]{:T(128)S(6)} %select_n.142, bf16[256,8,128]{2,1,0:T(8,128)(2,1)} %bitcast.670, ...), kind=kOutput, calls=%fused_computation.43 | convolution fusion | flops 270565120 | bytes 8397828 | tf_op jit(solution)/shard_map/dot_general | solution.py:40
  420.7 3.5 convolution_convert_fusion.9
  428.0 17.6 %reduce-scatter.17.cloned.1.call-done = bf16[64,256]{1,0:T(8,128)(2,1)} async-done(((bf16[256,256]{1,0:T(8,128)(2,1)}), bf16[64,256]{1,0:T(8,128)(2,1)}) %reduce-scatter.17.cloned.1.call-update) | async-done | bytes 32784 | tf_op jit(solution)/shard_map/reduce_scatter | solution.py:232
  (250 shorter events, 69.3 us)
Async XLA Ops:
  7.2 108.5 %copy-start = (bf16[1,2048,512]{2,1,0:T(8,128)(2,1)S(1)}, bf16[1,2048,512]{2,1,0:T(8,128)(2,1)}, u32[]{:S(2)}) copy-start(bf16[1,2048,512]{2,1,0:T(8,128)(2,1)} %param.24) | copy-start | bytes 6291460
  7.2 133.1 %reduce-scatter.7.cloned.1.call-start = ((), (), s32[]{:S(2)}) async-start(), calls=%async_computation.6 | async-start | bytes 163840 | tf_op jit(solution)/shard_map/reduce_scatter | solution.py:211
  9.5 106.2 %copy-start.26 = (pred[256,256]{0,1:T(8,128)(4,1)}, pred[256,256]{0,1:T(8,128)(4,1)S(1)}, u32[]{:S(2)}) copy-start(pred[256,256]{0,1:T(8,128)(4,1)S(1)} %iota_compare_fusion) | copy-start | bytes 196612
  9.6 84.3 %copy-start.49 = (bf16[1,256,256]{2,1,0:T(8,128)(2,1)S(1)}, bf16[1,256,256]{2,1,0:T(8,128)(2,1)}, u32[]{:S(2)}) copy-start(bf16[1,256,256]{2,1,0:T(8,128)(2,1)} %param.15) | copy-start | bytes 393220
  13.6 81.3 %copy-start.1 = (bf16[1,256,2048]{2,1,0:T(8,128)(2,1)S(1)}, bf16[1,256,2048]{2,1,0:T(8,128)(2,1)}, u32[]{:S(2)}) copy-start(bf16[1,256,2048]{2,1,0:T(8,128)(2,1)} %param.19) | copy-start | bytes 3145732
  107.6 4.0 copy-start.40
  107.6 4.1 copy-start.77
  121.6 83.0 %reduce-scatter.9.cloned.1.call-start = ((), (), s32[]{:S(2)}) async-start(), calls=%async_computation.7 | async-start | bytes 163840 | tf_op jit(solution)/shard_map/reduce_scatter | solution.py:211
  141.8 4.4 collective-permute-start
  144.2 19.5 %copy-start.66 = (f32[256]{0:T(256)}, f32[256]{0:T(256)S(1)}, u32[]{:S(2)}) copy-start(f32[256]{0:T(256)S(1)} %get-tuple-element.33) | copy-start | bytes 3076
  163.7 4.1 copy-start.15
  164.4 5.7 %copy-start.12 = (bf16[256,2048]{1,0:T(8,128)(2,1)}, bf16[256,2048]{1,0:T(8,128)(2,1)S(1)}, u32[]{:S(2)}) copy-start(bf16[256,2048]{1,0:T(8,128)(2,1)S(1)} %get-tuple-element.19) | copy-start | bytes 3145732
  164.4 6.2 %copy-start.14 = (bf16[256,2048]{1,0:T(8,128)(2,1)}, bf16[256,2048]{1,0:T(8,128)(2,1)S(1)}, u32[]{:S(2)}) copy-start(bf16[256,2048]{1,0:T(8,128)(2,1)S(1)} %get-tuple-element.20) | copy-start | bytes 3145732
  164.4 8.6 %copy-start.13 = (bf16[256,2048]{1,0:T(8,128)(2,1)}, bf16[256,2048]{1,0:T(8,128)(2,1)S(1)}, u32[]{:S(2)}) copy-start(bf16[256,2048]{1,0:T(8,128)(2,1)S(1)} %get-tuple-element.21) | copy-start | bytes 3145732
  173.0 4.1 copy-start.27
  185.6 106.6 %reduce-scatter.13.cloned.1.call-start = ((), (), s32[]{:S(2)}) async-start(), calls=%async_computation.9 | async-start | bytes 163840 | tf_op jit(solution)/shard_map/reduce_scatter | solution.py:232
  185.7 5.0 %copy-start.71 = (f32[256]{0:T(256)S(1)}, f32[256]{0:T(256)}, u32[]{:S(2)}) copy-start(f32[256]{0:T(256)} %get-tuple-element.74) | copy-start | bytes 3076
  185.7 5.6 %copy-start.22 = (bf16[256,256]{1,0:T(8,128)(2,1)S(1)}, bf16[256,256]{1,0:T(8,128)(2,1)}, u32[]{:S(2)}) copy-start(bf16[256,256]{1,0:T(8,128)(2,1)} %copy-done.21) | copy-start | bytes 393220
  205.5 3.1 collective-permute-start.1
  208.5 23.6 %copy-start.10 = (f32[256,256,8]{1,0,2:T(8,128)}, f32[256,256,8]{1,0,2:T(8,128)S(1)}, u32[]{:S(2)}) copy-start(f32[256,256,8]{1,0,2:T(8,128)S(1)} %fusion.142) | copy-start | bytes 6291460
  208.6 15.2 %copy-start.23 = (bf16[256,256]{1,0:T(8,128)(2,1)S(1)}, bf16[256,256]{1,0:T(8,128)(2,1)}, u32[]{:S(2)}) copy-start(bf16[256,256]{1,0:T(8,128)(2,1)} %copy-done.21) | copy-start | bytes 393220
  225.9 3.7 copy-start.16
  227.3 3.6 copy-start.20
  230.9 4.5 copy-start.8
  231.5 3.9 copy-start.64
  232.1 3.3 copy-start.53
  235.4 5.0 %copy-start.69 = (f32[8,256]{1,0:T(8,128)}, f32[8,256]{1,0:T(8,128)S(1)}, u32[]{:S(2)}) copy-start(f32[8,256]{1,0:T(8,128)S(1)} %get-tuple-element.5) | copy-start | bytes 24580
  240.4 4.1 copy-start.6
  240.4 4.1 copy-start.25
  240.4 4.1 copy-start.48
  244.6 3.6 copy-start.17
  257.2 3.6 copy-start.42
  257.2 3.6 copy-start.60
  257.3 3.6 copy-start.76
  263.7 5.1 %copy-start.67 = (f32[256]{0:T(256)S(1)}, f32[256]{0:T(256)}, u32[]{:S(2)}) copy-start(f32[256]{0:T(256)} %copy-done.66) | copy-start | bytes 3076
  263.7 5.1 %copy-start.74 = (f32[256]{0:T(256)S(1)}, f32[256]{0:T(256)}, u32[]{:S(2)}) copy-start(f32[256]{0:T(256)} %get-tuple-element.32) | copy-start | bytes 3076
  268.8 3.6 copy-start.70
  272.3 40.3 %copy-start.29 = (pred[256,256]{0,1:T(8,128)(4,1)S(1)}, pred[256,256]{0,1:T(8,128)(4,1)}, u32[]{:S(2)}) copy-start(pred[256,256]{0,1:T(8,128)(4,1)} %copy-done.26) | copy-start | bytes 196612
  272.3 92.7 %reduce-scatter.15.cloned.1.call-start = ((), (), s32[]{:S(2)}) async-start(), calls=%async_computation.10 | async-start | bytes 163840 | tf_op jit(solution)/shard_map/reduce_scatter | solution.py:232
  293.1 24.5 %copy-start.51 = (bf16[64,256]{1,0:T(8,128)(2,1)}, bf16[64,256]{1,0:T(8,128)(2,1)S(1)}, u32[]{:S(2)}) copy-start(bf16[64,256]{1,0:T(8,128)(2,1)S(1)} %add_convert_fusion.2) | copy-start | bytes 98308
  293.1 3.1 collective-permute-start.2
  317.6 4.1 copy-start.5
  317.6 4.1 copy-start.24
  331.9 3.6 copy-start.43
  331.9 3.6 copy-start.58
  331.9 3.6 copy-start.75
  343.4 3.6 copy-start.45
  343.4 3.6 copy-start.56
  347.0 78.7 %reduce-scatter.11.cloned.1.call-start = ((), (), s32[]{:S(2)}) async-start(), calls=%async_computation.8 | async-start | bytes 163840 | tf_op jit(solution)/shard_map/reduce_scatter | solution.py:211
  350.1 35.7 %copy-start.30 = (pred[256,256]{0,1:T(8,128)(4,1)S(1)}, pred[256,256]{0,1:T(8,128)(4,1)}, u32[]{:S(2)}) copy-start(pred[256,256]{0,1:T(8,128)(4,1)} %copy-done.26) | copy-start | bytes 196612
  350.1 35.7 %copy-start.68 = (f32[8,256]{1,0:T(8,128)S(1)}, f32[8,256]{1,0:T(8,128)}, u32[]{:S(2)}) copy-start(f32[8,256]{1,0:T(8,128)} %get-tuple-element.4) | copy-start | bytes 24580
  365.9 25.3 %copy-start.52 = (bf16[64,256]{1,0:T(8,128)(2,1)}, bf16[64,256]{1,0:T(8,128)(2,1)S(1)}, u32[]{:S(2)}) copy-start(bf16[64,256]{1,0:T(8,128)(2,1)S(1)} %add_convert_fusion.1) | copy-start | bytes 98308
  365.9 3.4 collective-permute-start.3
  391.2 4.0 copy-start.9
  391.2 4.0 copy-start.35
  391.2 4.0 copy-start.54
  402.3 5.0 %copy-start.55 = (f32[256,8]{0,1:T(8,128)S(1)}, f32[256,8]{0,1:T(8,128)}, u32[]{:S(2)}) copy-start(f32[256,8]{0,1:T(8,128)} %get-tuple-element.13) | copy-start | bytes 24580
  407.2 38.3 %reduce-scatter.17.cloned.1.call-start = ((), (), s32[]{:S(2)}) async-start(), calls=%async_computation.11 | async-start | bytes 163840 | tf_op jit(solution)/shard_map/reduce_scatter | solution.py:232
  409.1 3.6 copy-start.36
  409.1 3.6 copy-start.41
  409.1 3.6 copy-start.73
  415.6 5.1 %copy-start.62 = (f32[256]{0:T(256)S(1)}, f32[256]{0:T(256)}, u32[]{:S(2)}) copy-start(f32[256]{0:T(256)} %copy-done.61) | copy-start | bytes 3076
  415.6 5.1 %copy-start.72 = (f32[256]{0:T(256)S(1)}, f32[256]{0:T(256)}, u32[]{:S(2)}) copy-start(f32[256]{0:T(256)} %get-tuple-element.24) | copy-start | bytes 3076
  420.7 3.5 copy-start.38
  (24 other events, 42.4 us)
Sparse Core Ops, SparseCore 0:
  121.7 18.5 reduce-scatter.6
  185.7 18.8 reduce-scatter.8
  272.5 19.7 reduce-scatter.12
  347.1 17.8 reduce-scatter.14
  407.3 18.2 reduce-scatter.10
  427.8 17.6 reduce-scatter.16
where the time goes:
time: 463 us; the launch traced here: 455 us
  matrix products  156 us (34%)
  blocking collectives  133 us (29%)
  waiting for transfers between devices  69 us (15%)
  other arithmetic  47.6 us (10%)
  local copies, waits for them, and re-layouts  27.8 us (6%)
  between operations  15.2 us (3%)
  starting transfers between devices  6.18 us (1%)
    psum x1, blocking collectives, shards(): embedded = lax.psum(picked, ('segment', 'head')).astype(jnp.bfloat16)  78 us
    dot_general x15, matrix products, narrow_back(): lax.dot_general(former, latter, (((1,), (1,)), ((), ())), preferred_eleme...  51.8 us
    reduce_scatter x3, waiting for transfers between devices, shards(): lax.psum_scatter(partial_back.astype(jnp.bfloat16), 'head', scatter_dimen...  46.7 us
    all_gather x2, blocking collectives, shards(): forward_recv = lax.all_gather(arrived, 'head', axis=0, tiled=True)  27.6 us
    all_gather x2, blocking collectives, shards(): backward_recv = lax.all_gather(arrived_back, 'head', axis=0, tiled=True)  27.1 us
    reduce_scatter x3, waiting for transfers between devices, shards(): lax.psum_scatter(partial_value.astype(jnp.bfloat16), 'head', scatter_dime...  21.6 us
    dot_general x6, matrix products, probabilities(): jnp.einsum('iknd,jkd->knij', grouped, k_hat, preferred_element_type=jnp.f...  15.6 us
    dot_general x3, matrix products, section_backward(): jnp.einsum('iknd,jkd->knij', grad_attended, values, preferred_element_typ...  15.3 us
  transfers between devices with their start and end apart: 10, of which 7 were waited for; matrix products, arithmetic and copies ran while one was open for 11% of the time, Pallas kernels for 0%

commit v1 on v0

--- a/solution.py
+++ b/solution.py
@@ -3,6 +3,7 @@
 import jax.numpy as jnp
 from jax import lax
 from jax.sharding import PartitionSpec as P
+from jax.lax import all_gather
 
 QUERY_HEADS = 32
 KEY_VALUE_HEADS = 4
@@ -184,7 +185,13 @@
         jnp.float32
     )
     picked = jnp.where(inside[:, None], looked, 0.0)
-    embedded = lax.psum(picked, ("segment", "head")).astype(jnp.bfloat16)
+
+    def _state_chunk(z, which_axis):
+        formed = all_gather(z, which_axis)
+        placed = jnp.sum(formed, axis=0)
+        return placed
+
+    embedded = _state_chunk(picked, ("segment", "head")).astype(jnp.bfloat16)
     tick_count = token_ids.shape[0]
     span_rows = token_ids.shape[1]
     embedded = embedded.reshape(tick_count, span_rows, -1)

time: 463 us -> 478 us (1.032)
  waiting for transfers between devices: 69 us -> 163 us
  blocking collectives: 133 us -> 54.5 us
    all_gather x0 -> x1, waiting for transfers between devices: none -> 86.1 us  [_state_chunk(): formed = all_gather(z, which_axis)]
    psum x1 -> x0, blocking collectives: 78 us -> none  [shards(): embedded = lax.psum(picked, ('segment', 'head')).astype(jnp.bfloat16)]
    reduce_scatter x3, waiting for transfers between devices: 21.6 us -> 28.8 us  [shards(): lax.psum_scatter(partial_value.astype(jnp.bfloat16), 'head', scatter_dime...]
    reduce_sum x0 -> x1, other arithmetic: none -> 6.27 us  [_state_chunk(): placed = jnp.sum(formed, axis=0)]
  transfers between devices with their start and end apart: 10 -> 11, of which waited for: 7 -> 9; matrix products, arithmetic and copies ran while one was open for 11% -> 13% of each run, Pallas kernels for 0% -> 0%
where the time goes in v1:
time: 478 us; the launch traced here: 469 us
  waiting for transfers between devices  163 us (34%)
  matrix products  154 us (32%)
  blocking collectives  54.5 us (11%)
  other arithmetic  51.3 us (11%)
  local copies, waits for them, and re-layouts  25.4 us (5%)
  between operations  15.2 us (3%)
  starting transfers between devices  5.63 us (1%)
    all_gather x1, waiting for transfers between devices, _state_chunk(): formed = all_gather(z, which_axis)  86.1 us
    dot_general x15, matrix products, narrow_back(): lax.dot_general(former, latter, (((1,), (1,)), ((), ())), preferred_eleme...  50.9 us
    reduce_scatter x3, waiting for transfers between devices, shards(): lax.psum_scatter(partial_back.astype(jnp.bfloat16), 'head', scatter_dimen...  46.8 us
    reduce_scatter x3, waiting for transfers between devices, shards(): lax.psum_scatter(partial_value.astype(jnp.bfloat16), 'head', scatter_dime...  28.8 us
    all_gather x2, blocking collectives, shards(): forward_recv = lax.all_gather(arrived, 'head', axis=0, tiled=True)  27.4 us
    all_gather x2, blocking collectives, shards(): backward_recv = lax.all_gather(arrived_back, 'head', axis=0, tiled=True)  27.1 us
    dot_general x6, matrix products, probabilities(): jnp.einsum('iknd,jkd->knij', grouped, k_hat, preferred_element_type=jnp.f...  15.5 us
    dot_general x3, matrix products, section_backward(): jnp.einsum('iknd,jkd->knij', grad_attended, values, preferred_element_typ...  15.4 us
  transfers between devices with their start and end apart: 11, of which 9 were waited for; matrix products, arithmetic and copies ran while one was open for 13% of the time, Pallas kernels for 0%

profile of v1, /device:TPU:0, one launch (start us, length us, event | category | flops | bytes accessed | tf_op | source)
XLA Modules:
  0.0 468.7 jit_solution(1691144233359509745)
XLA Ops:
  9.5 3.2 gather_fusion
  14.1 3.8 fusion.32
  20.2 6.7 %copy.123 = bf16[1024,2048]{1,0:T(8,128)(2,1)} copy(bf16[1024,2048]{0,1:T(8,128)(2,1)} %bitcast.663) | data formatting | bytes 8388608 | tf_op jit(solution)/shard_map/dot_general | solution.py:58
  29.2 1.9 fusion.155
  31.2 86.1 %all-gather.2.cloned.1.call-done = f32[16,768,256]{2,1,0:T(8,128)} async-done(((f32[1,768,256]{2,1,0:T(8,128)}), f32[16,768,256]{2,1,0:T(8,128)}) %all-gather.2.cloned.1.call-update) | async-done | bytes 12582928 | tf_op jit(solution)/shard_map/all_gather | solution.py:190
  117.3 6.3 %reduce_sum.357 = bf16[768,256]{1,0:T(8,128)(2,1)} reduce(f32[16,768,256]{2,1,0:T(8,128)} %all-gather.2.cloned.1.call-done, f32[]{:T(128)} %constant.94.clone.1), dimensions={0}, to_apply=%region_0.1 | reduce | flops 2949120 | bytes 12976132 | tf_op jit(solution)/shard_map/reduce_sum | solution.py:191
  125.4 2.1 multiply_reduce_fusion.23
  129.2 1.9 fusion.23
  131.1 3.7 convolution_convert_fusion.5
  134.8 2.2 convolution_convert_fusion.8
  137.0 2.7 multiply_reduce_fusion.5
  140.8 14.1 %reduce-scatter.7.cloned.1.call-done = bf16[64,256]{1,0:T(8,128)(2,1)} async-done(((bf16[256,256]{1,0:T(8,128)(2,1)}), bf16[64,256]{1,0:T(8,128)(2,1)}) %reduce-scatter.7.cloned.1.call-update) | async-done | bytes 32784 | tf_op jit(solution)/shard_map/reduce_scatter | solution.py:218
  157.9 13.6 %all_gather.17 = bf16[256,256]{1,0:T(8,128)(2,1)S(1)} all-gather(bf16[64,256]{1,0:T(8,128)(2,1)S(1)} %collective-permute-done), channel_id=1, replica_groups=mesh['groups'=2,'segment'=4,'head'=4] {'head'}, dimensions={0}, use_global_device_ids=true | all-gather | bytes 163840 | tf_op jit(solution)/shard_map/all_gather | solution.py:227
  179.3 2.3 multiply_reduce_fusion.12
  184.5 2.9 multiply_reduce_fusion.14
  188.6 2.5 fusion.24
  191.1 3.7 convolution_convert_fusion.4
  194.9 2.2 convolution_convert_fusion.7
  199.1 3.1 fusion.141
  203.8 14.5 %reduce-scatter.9.cloned.1.call-done = bf16[64,256]{1,0:T(8,128)(2,1)} async-done(((bf16[256,256]{1,0:T(8,128)(2,1)}), bf16[64,256]{1,0:T(8,128)(2,1)}) %reduce-scatter.9.cloned.1.call-update) | async-done | bytes 32784 | tf_op jit(solution)/shard_map/reduce_scatter | solution.py:218
  220.4 1.8 fusion.142
  222.2 13.8 %all_gather.18 = bf16[256,256]{1,0:T(8,128)(2,1)S(1)} all-gather(bf16[64,256]{1,0:T(8,128)(2,1)S(1)} %collective-permute-done.1), channel_id=1, replica_groups=mesh['groups'=2,'segment'=4,'head'=4] {'head'}, dimensions={0}, use_global_device_ids=true | all-gather | bytes 163840 | tf_op jit(solution)/shard_map/all_gather | solution.py:227
  240.9 2.3 multiply_reduce_fusion.18
  245.8 3.2 fusion.31
  249.1 5.0 %fusion.19 = (f32[8,256]{1,0:T(8,128)}, f32[256,256,8]{1,0,2:T(8,128)}) fusion(f32[8,256]{1,0:T(8,128)S(1)} %get-tuple-element.5, f32[256,256,8]{1,0,2:T(8,128)} %fusion.141, pred[256,256]{0,1:T(8,128)(4,1)S(1)} %copy-done.30, bf16[256,2048]{1,0:T(8,128)(2,1)} %copy-done.14, bf16[1,2048,512]{2,1,0:T(8,128)(2,1)S(1)} %copy-done, s32[]{:T(128)S(6)} %select_n.156, ...), kind=kOutput, calls=%fused_computation.38 | convolution fusion | flops 271087616 | bytes 6373380 | tf_op jit(solution)/shard_map/iknd,jkd->knij/dot_general | solution.py:111
  254.1 4.1 convert_bitcast_fusion.2
  259.9 1.9 multiply_reduce_fusion.13
  261.8 2.9 multiply_reduce_fusion.15
  264.7 3.0 copy.101
  269.1 1.7 subtract_convert_fusion.8
  270.9 3.6 fusion.4
  274.5 2.9 convolution_add_fusion.5
  277.4 5.1 %multiply_reduce_fusion.4 = (f32[256]{0:T(256)S(1)}, f32[256,2048]{1,0:T(8,128)}) fusion(f32[256,2048]{1,0:T(8,128)} %get-tuple-element.49, f32[2048]{0:T(1024)S(1)} %bitcast.682, f32[256,2048]{1,0:T(8,128)} %convolution_add_fusion.5, bf16[1,2048,512]{2,1,0:T(8,128)(2,1)S(1)} %copy-done, s32[]{:T(128)S(6)} %select_n.156, ...), kind=kOutput, calls=%fused_computation.51 | convolution fusion | flops 270565120 | bytes 8397828 | tf_op jit(solution)/shard_map/dot_general | solution.py:41
  282.5 3.5 convolution_convert_fusion.11
  286.6 3.0 multiply_reduce_fusion.21
  289.7 16.3 %reduce-scatter.13.cloned.1.call-done = bf16[64,256]{1,0:T(8,128)(2,1)} async-done(((bf16[256,256]{1,0:T(8,128)(2,1)}), bf16[64,256]{1,0:T(8,128)(2,1)}) %reduce-scatter.13.cloned.1.call-update) | async-done | bytes 32784 | tf_op jit(solution)/shard_map/reduce_scatter | solution.py:239
  309.9 13.5 %all_gather.19 = bf16[256,256]{1,0:T(8,128)(2,1)S(1)} all-gather(bf16[64,256]{1,0:T(8,128)(2,1)S(1)} %collective-permute-done.2), channel_id=1, replica_groups=mesh['groups'=2,'segment'=4,'head'=4] {'head'}, dimensions={0}, use_global_device_ids=true | all-gather | bytes 163840 | tf_op jit(solution)/shard_map/all_gather | solution.py:248
  324.1 2.2 convolution_convert_fusion.1
  326.4 5.0 %fusion.15 = (f32[8,256]{1,0:T(8,128)}, f32[256,256,8]{1,0,2:T(8,128)}) fusion(f32[8,256]{1,0:T(8,128)} %get-tuple-element.6, f32[256,256,8]{1,0,2:T(8,128)} %copy-done.10, pred[256,256]{0,1:T(8,128)(4,1)S(1)} %copy-done.31, bf16[256,2048]{1,0:T(8,128)(2,1)} %copy-done.13, bf16[1,2048,512]{2,1,0:T(8,128)(2,1)S(1)} %copy-done, s32[]{:T(128)S(6)} %select_n.156, ...), kind=kOutput, calls=%fused_computation.32 | convolution fusion | flops 271087616 | bytes 6373380 | tf_op jit(solution)/shard_map/iknd,jkd->knij/dot_general | solution.py:111
  331.4 4.0 convert_bitcast_fusion.1
  337.1 1.9 multiply_reduce_fusion.11
  339.9 2.7 copy.107
  343.9 1.8 subtract_convert_fusion.7
  345.7 3.6 fusion.2
  349.3 2.9 convolution_add_fusion.3
  352.2 5.1 %multiply_reduce_fusion.2 = (f32[256]{0:T(256)S(1)}, f32[256,2048]{1,0:T(8,128)}) fusion(f32[256,2048]{1,0:T(8,128)} %copy-done.3, f32[2048]{0:T(1024)S(1)} %bitcast.683, f32[256,2048]{1,0:T(8,128)} %convolution_add_fusion.3, bf16[1,2048,512]{2,1,0:T(8,128)(2,1)S(1)} %copy-done, s32[]{:T(128)S(6)} %select_n.156, bf16[256,8,128]{2,1,0:T(8,128)(2,1)} %bitcast.675, ...), kind=kOutput, calls=%fused_computation.47 | convolution fusion | flops 270565120 | bytes 8397828 | tf_op jit(solution)/shard_map/dot_general | solution.py:41
  357.3 3.5 convolution_convert_fusion.10
  360.9 3.0 fusion.101
  363.9 2.0 fusion.195
  366.0 12.9 %reduce-scatter.15.cloned.1.call-done = bf16[64,256]{1,0:T(8,128)(2,1)} async-done(((bf16[256,256]{1,0:T(8,128)(2,1)}), bf16[64,256]{1,0:T(8,128)(2,1)}) %reduce-scatter.15.cloned.1.call-update) | async-done | bytes 32784 | tf_op jit(solution)/shard_map/reduce_scatter | solution.py:239
  381.2 1.9 fusion.268
  383.1 13.6 %all_gather.20 = bf16[256,256]{1,0:T(8,128)(2,1)S(1)} all-gather(bf16[64,256]{1,0:T(8,128)(2,1)S(1)} %collective-permute-done.3), channel_id=1, replica_groups=mesh['groups'=2,'segment'=4,'head'=4] {'head'}, dimensions={0}, use_global_device_ids=true | all-gather | bytes 163840 | tf_op jit(solution)/shard_map/all_gather | solution.py:248
  397.4 2.2 convolution_convert_fusion
  399.6 5.4 %fusion.11 = (f32[8,256]{1,0:T(8,128)S(1)}, f32[8,256]{1,0:T(8,128)S(1)}, f32[256,256,8]{1,0,2:T(8,128)}) fusion(f32[8,256]{1,0:T(8,128)S(1)} %copy-done.70, f32[256,256,8]{1,0,2:T(8,128)} %get-tuple-element.76, pred[256,256]{0,1:T(8,128)(4,1)S(1)} %copy-done.32, f32[256,256,8]{1,0,2:T(8,128)} %fusion.101, bf16[256,2048]{1,0:T(8,128)(2,1)} %copy-done.22, ...), kind=kOutput, calls=%fused_computation.26 | convolution fusion | flops 272658432 | bytes 8478724 | tf_op jit(solution)/shard_map/iknd,jkd->knij/dot_general | solution.py:111
  405.1 4.1 convert_bitcast_fusion
  412.5 3.7 convolution_convert_fusion.3
  416.3 2.7 copy.113
  418.9 2.2 convolution_convert_fusion.6
  421.2 1.8 subtract_convert_fusion.6
  423.0 3.6 fusion.6
  426.6 2.8 convolution_add_fusion.1
  429.5 5.1 %multiply_reduce_fusion = (f32[256]{0:T(256)S(1)}, f32[256,2048]{1,0:T(8,128)}) fusion(f32[256,2048]{1,0:T(8,128)} %copy-done.2, f32[2048]{0:T(1024)S(1)} %bitcast.684, f32[256,2048]{1,0:T(8,128)} %convolution_add_fusion.1, bf16[1,2048,512]{2,1,0:T(8,128)(2,1)S(1)} %copy-done, s32[]{:T(128)S(6)} %select_n.156, bf16[256,8,128]{2,1,0:T(8,128)(2,1)} %bitcast.674, ...), kind=kOutput, calls=%fused_computation.43 | convolution fusion | flops 270565120 | bytes 8397828 | tf_op jit(solution)/shard_map/dot_general | solution.py:41
  434.6 3.5 convolution_convert_fusion.9
  441.9 17.6 %reduce-scatter.17.cloned.1.call-done = bf16[64,256]{1,0:T(8,128)(2,1)} async-done(((bf16[256,256]{1,0:T(8,128)(2,1)}), bf16[64,256]{1,0:T(8,128)(2,1)}) %reduce-scatter.17.cloned.1.call-update) | async-done | bytes 32784 | tf_op jit(solution)/shard_map/reduce_scatter | solution.py:239
  (255 shorter events, 65.6 us)
Async XLA Ops:
  7.2 123.9 %copy-start = (bf16[1,2048,512]{2,1,0:T(8,128)(2,1)S(1)}, bf16[1,2048,512]{2,1,0:T(8,128)(2,1)}, u32[]{:S(2)}) copy-start(bf16[1,2048,512]{2,1,0:T(8,128)(2,1)} %param.24) | copy-start | bytes 6291460
  7.2 110.1 %all-gather.2.cloned.1.call-start = ((), (), s32[]{:S(2)}) async-start(), calls=%async_computation.6 | async-start | bytes 13369344 | tf_op jit(solution)/shard_map/all_gather | solution.py:190
  14.0 140.9 %reduce-scatter.7.cloned.1.call-start = ((), (), s32[]{:S(2)}) async-start(), calls=%async_computation.7 | async-start | bytes 163840 | tf_op jit(solution)/shard_map/reduce_scatter | solution.py:218
  14.1 3.8 copy-start.46
  20.2 7.3 %copy-start.1 = (bf16[1,256,2048]{2,1,0:T(8,128)(2,1)S(1)}, bf16[1,256,2048]{2,1,0:T(8,128)(2,1)}, u32[]{:S(2)}) copy-start(bf16[1,256,2048]{2,1,0:T(8,128)(2,1)} %param.19) | copy-start | bytes 3145732
  125.4 3.8 copy-start.20
  137.0 81.2 %reduce-scatter.9.cloned.1.call-start = ((), (), s32[]{:S(2)}) async-start(), calls=%async_computation.8 | async-start | bytes 163840 | tf_op jit(solution)/shard_map/reduce_scatter | solution.py:218
  155.7 2.1 collective-permute-start
  157.6 17.6 %copy-start.68 = (f32[256]{0:T(256)}, f32[256]{0:T(256)S(1)}, u32[]{:S(2)}) copy-start(f32[256]{0:T(256)S(1)} %get-tuple-element.33) | copy-start | bytes 3076
  175.2 4.1 copy-start.17
  175.9 5.7 %copy-start.13 = (bf16[256,2048]{1,0:T(8,128)(2,1)}, bf16[256,2048]{1,0:T(8,128)(2,1)S(1)}, u32[]{:S(2)}) copy-start(bf16[256,2048]{1,0:T(8,128)(2,1)S(1)} %get-tuple-element.19) | copy-start | bytes 3145732
  175.9 6.2 %copy-start.15 = (bf16[256,2048]{1,0:T(8,128)(2,1)}, bf16[256,2048]{1,0:T(8,128)(2,1)S(1)}, u32[]{:S(2)}) copy-start(bf16[256,2048]{1,0:T(8,128)(2,1)S(1)} %get-tuple-element.20) | copy-start | bytes 3145732
  175.9 8.6 %copy-start.14 = (bf16[256,2048]{1,0:T(8,128)(2,1)}, bf16[256,2048]{1,0:T(8,128)(2,1)S(1)}, u32[]{:S(2)}) copy-start(bf16[256,2048]{1,0:T(8,128)(2,1)S(1)} %get-tuple-element.21) | copy-start | bytes 3145732
  184.5 4.1 copy-start.29
  197.1 108.9 %reduce-scatter.13.cloned.1.call-start = ((), (), s32[]{:S(2)}) async-start(), calls=%async_computation.10 | async-start | bytes 163840 | tf_op jit(solution)/shard_map/reduce_scatter | solution.py:239
  197.1 5.1 %copy-start.73 = (f32[256]{0:T(256)S(1)}, f32[256]{0:T(256)}, u32[]{:S(2)}) copy-start(f32[256]{0:T(256)} %get-tuple-element.74) | copy-start | bytes 3076
  197.1 5.6 %copy-start.24 = (bf16[256,256]{1,0:T(8,128)(2,1)S(1)}, bf16[256,256]{1,0:T(8,128)(2,1)}, u32[]{:S(2)}) copy-start(bf16[256,256]{1,0:T(8,128)(2,1)} %copy-done.23) | copy-start | bytes 393220
  219.1 3.1 copy-start.52
  219.1 3.1 collective-permute-start.1
  222.2 23.6 %copy-start.10 = (f32[256,256,8]{1,0,2:T(8,128)}, f32[256,256,8]{1,0,2:T(8,128)S(1)}, u32[]{:S(2)}) copy-start(f32[256,256,8]{1,0,2:T(8,128)S(1)} %fusion.142) | copy-start | bytes 6291460
  222.2 15.3 %copy-start.25 = (bf16[256,256]{1,0:T(8,128)(2,1)S(1)}, bf16[256,256]{1,0:T(8,128)(2,1)}, u32[]{:S(2)}) copy-start(bf16[256,256]{1,0:T(8,128)(2,1)} %copy-done.23) | copy-start | bytes 393220
  239.5 3.7 copy-start.18
  240.9 3.6 copy-start.22
  244.6 4.5 copy-start.8
  245.2 3.9 copy-start.66
  245.8 3.3 copy-start.55
  249.0 5.0 %copy-start.71 = (f32[8,256]{1,0:T(8,128)}, f32[8,256]{1,0:T(8,128)S(1)}, u32[]{:S(2)}) copy-start(f32[8,256]{1,0:T(8,128)S(1)} %get-tuple-element.5) | copy-start | bytes 24580
  254.0 4.1 copy-start.6
  254.0 4.1 copy-start.27
  254.0 4.1 copy-start.50
  258.2 3.6 copy-start.19
  270.9 3.6 copy-start.44
  270.9 3.6 copy-start.62
  270.9 3.6 copy-start.78
  277.4 5.1 %copy-start.69 = (f32[256]{0:T(256)S(1)}, f32[256]{0:T(256)}, u32[]{:S(2)}) copy-start(f32[256]{0:T(256)} %copy-done.68) | copy-start | bytes 3076
  277.4 5.1 %copy-start.76 = (f32[256]{0:T(256)S(1)}, f32[256]{0:T(256)}, u32[]{:S(2)}) copy-start(f32[256]{0:T(256)} %get-tuple-element.32) | copy-start | bytes 3076
  282.5 3.6 copy-start.72
  286.0 40.4 %copy-start.31 = (pred[256,256]{0,1:T(8,128)(4,1)S(1)}, pred[256,256]{0,1:T(8,128)(4,1)}, u32[]{:S(2)}) copy-start(pred[256,256]{0,1:T(8,128)(4,1)} %iota_compare_fusion) | copy-start | bytes 196612
  286.0 92.9 %reduce-scatter.15.cloned.1.call-start = ((), (), s32[]{:S(2)}) async-start(), calls=%async_computation.11 | async-start | bytes 163840 | tf_op jit(solution)/shard_map/reduce_scatter | solution.py:239
  306.8 24.5 %copy-start.53 = (bf16[64,256]{1,0:T(8,128)(2,1)}, bf16[64,256]{1,0:T(8,128)(2,1)S(1)}, u32[]{:S(2)}) copy-start(bf16[64,256]{1,0:T(8,128)(2,1)S(1)} %add_convert_fusion.2) | copy-start | bytes 98308
  306.8 3.1 collective-permute-start.2
  331.4 4.0 copy-start.5
  331.4 4.0 copy-start.26
  345.7 3.6 copy-start.45
  345.7 3.6 copy-start.60
  345.7 3.6 copy-start.77
  357.3 3.6 copy-start.47
  357.3 3.6 copy-start.58
  360.9 78.7 %reduce-scatter.11.cloned.1.call-start = ((), (), s32[]{:S(2)}) async-start(), calls=%async_computation.9 | async-start | bytes 163840 | tf_op jit(solution)/shard_map/reduce_scatter | solution.py:218
  363.9 35.7 %copy-start.32 = (pred[256,256]{0,1:T(8,128)(4,1)S(1)}, pred[256,256]{0,1:T(8,128)(4,1)}, u32[]{:S(2)}) copy-start(pred[256,256]{0,1:T(8,128)(4,1)} %iota_compare_fusion) | copy-start | bytes 196612
  363.9 35.7 %copy-start.70 = (f32[8,256]{1,0:T(8,128)S(1)}, f32[8,256]{1,0:T(8,128)}, u32[]{:S(2)}) copy-start(f32[8,256]{1,0:T(8,128)} %get-tuple-element.4) | copy-start | bytes 24580
  379.7 25.3 %copy-start.54 = (bf16[64,256]{1,0:T(8,128)(2,1)}, bf16[64,256]{1,0:T(8,128)(2,1)S(1)}, u32[]{:S(2)}) copy-start(bf16[64,256]{1,0:T(8,128)(2,1)S(1)} %add_convert_fusion.1) | copy-start | bytes 98308
  379.7 3.4 collective-permute-start.3
  405.1 4.1 copy-start.9
  405.1 4.1 copy-start.38
  405.1 4.1 copy-start.56
  416.3 5.0 %copy-start.57 = (f32[256,8]{0,1:T(8,128)S(1)}, f32[256,8]{0,1:T(8,128)}, u32[]{:S(2)}) copy-start(f32[256,8]{0,1:T(8,128)} %get-tuple-element.13) | copy-start | bytes 24580
  421.1 38.4 %reduce-scatter.17.cloned.1.call-start = ((), (), s32[]{:S(2)}) async-start(), calls=%async_computation.12 | async-start | bytes 163840 | tf_op jit(solution)/shard_map/reduce_scatter | solution.py:239
  423.0 3.6 copy-start.39
  423.0 3.6 copy-start.43
  423.0 3.6 copy-start.75
  429.5 5.1 %copy-start.64 = (f32[256]{0:T(256)S(1)}, f32[256]{0:T(256)}, u32[]{:S(2)}) copy-start(f32[256]{0:T(256)} %copy-done.63) | copy-start | bytes 3076
  429.5 5.1 %copy-start.74 = (f32[256]{0:T(256)S(1)}, f32[256]{0:T(256)}, u32[]{:S(2)}) copy-start(f32[256]{0:T(256)} %get-tuple-element.24) | copy-start | bytes 3076
  434.5 3.5 copy-start.41
  (26 other events, 43.6 us)
Sparse Core Ops, SparseCore 0:
  14.1 103.1 all-gather.1
  137.1 17.6 reduce-scatter.6
  197.2 20.9 reduce-scatter.8
  286.1 19.8 reduce-scatter.12
  361.0 17.8 reduce-scatter.14
  421.3 18.2 reduce-scatter.10
  441.8 17.6 reduce-scatter.16
